TPU v7x, 256 devices: a whole 4x4x8 slice. The times are simulated.
256 devices in a mesh: dp: 2 (over core), ctx: 128 (over x, z, y).
Axes of the slice: x: 4, y: 4, z: 8, core: 2. Of those that a mesh axis runs over, the one named last changes fastest.
Arguments:
- queries: bfloat16 [2, 16384, 2048], P('dp', 'ctx'), may hold values from -6 to 6
- keys: bfloat16 [2, 16384, 2048], P('dp', 'ctx'), may hold values from -6 to 6
- values: bfloat16 [2, 16384, 2048], P('dp', 'ctx'), may hold values from -6 to 6
- doc_ids: int32 [2, 256], P('dp', 'ctx'), may hold values from 0 to 7, never falling along the last dimension, each value on 1 to 64 neighbouring positions
- feat_weight: bfloat16 [128, 160], replicated, may hold values from -0.5 to 0.5
- out_grad: bfloat16 [2, 16384, 2048], P('dp', 'ctx'), may hold values from -6 to 6
Outputs:
- out: float32 [2, 16384, 2048], P('dp', 'ctx')
- query_grad: float32 [2, 16384, 2048], P('dp', 'ctx')
- key_grad: float32 [2, 16384, 2048], P('dp', 'ctx')
- value_grad: float32 [2, 16384, 2048], P('dp', 'ctx')
- new_weight: float32 [128, 160], replicated
Inputs may be any that keep to these rules, and one draw needn't show every extreme that they name: `doc_ids`: along each sequence the ids never fall; every id names one run of 1 to 64 blocks, and one run has exactly 64 blocks.
All inputs are finite; a program needn't handle non-finite values.
Results may differ from a plain program's by a relative error of at most 0.015.
Values sent between devices are 32-bit elements; how exact they have to be, the bound alone decides.
No kernel may reach another device: no remote copies, remote signals or barrier semaphores. Data moves between devices by JAX's collectives and lax.ppermute only.
A program may use at most 64 MiB of HBM per device.

v0:
```python
import math
import jax
import jax.numpy as jnp
from jax import lax
from jax.sharding import PartitionSpec as P

H = 16
DH = 128
F = 160
BLOCK = 64
HIGH = lax.Precision.HIGHEST
RATE = 0.5
EPSILON = 1e-06


def passed_along(array, axis, by):
    length = lax.axis_size(axis)
    pairs = [(i, i + by) for i in range(length) if 0 <= i + by < length]
    return lax.ppermute(array, axis, pairs)


def features(proj):
    return (1.0 + proj + 0.5 * proj * proj).astype(jnp.bfloat16)


def pack_parts(parts):
    return jnp.concatenate([part.reshape(-1) for part in parts])


def unpack_parts(packed, shapes):
    result = []
    offset = 0
    for shape in shapes:
        length = math.prod(shape)
        result.append(packed[offset : offset + length].reshape(shape))
        offset = offset + length
    return result


def chain_combine(earlier, later):
    joined = later[0] == earlier[0]
    merged = later[1:] + jnp.where(joined, earlier[1:], jnp.zeros_like(earlier[1:]))
    return jnp.concatenate([later[:1], merged])


def prefix(packed, reverse, mover):
    count = lax.axis_size("ctx")
    index = lax.axis_index("ctx")
    blank = jnp.zeros_like(packed).at[0].set(-1.0)
    sign = -1 if reverse else 1

    def valid(step):
        if reverse:
            return index < count - step
        return index >= step

    total = jnp.where(valid(1), mover(packed, sign), blank)
    step = 1
    while step < count:
        got = mover(total, sign * step)
        total = jnp.where(valid(step), chain_combine(got, total), total)
        step = step * 2
    return total


def state_mover(value, by):
    return passed_along(value, "ctx", by)


def adjoint_mover(value, by):
    return passed_along(value, "ctx", by)


def shards(queries, keys, values, doc_ids, feat_weight, out_grad):
    tokens = queries.shape[1]
    query3 = queries.reshape(tokens, H, DH)
    key3 = keys.reshape(tokens, H, DH)
    value3 = values.reshape(tokens, H, DH)
    grad3 = out_grad.reshape(tokens, H, DH).astype(jnp.float32)
    blocks = doc_ids.shape[1]
    docs = jnp.broadcast_to(doc_ids[0][:, None], (blocks, BLOCK)).reshape(tokens)
    doc_float = docs.astype(jnp.float32)
    proj_q = jnp.einsum("thd,df->thf", query3, feat_weight, preferred_element_type=jnp.float32)
    proj_k = jnp.einsum("thd,df->thf", key3, feat_weight, preferred_element_type=jnp.float32)
    feat_q = features(proj_q)
    feat_k = features(proj_k)
    order = jnp.arange(tokens)
    mask = jnp.logical_and(order[None, :] <= order[:, None], docs[None, :] == docs[:, None]).astype(
        jnp.float32
    )
    raw = jnp.einsum("thf,shf->hts", feat_q, feat_k, preferred_element_type=jnp.float32)
    probs = (raw * mask[None]).astype(jnp.bfloat16)
    num_local = jnp.einsum("hts,shd->thd", probs, value3, preferred_element_type=jnp.float32)
    den_local = jnp.sum(probs, axis=2, dtype=jnp.float32).T
    feat_qf = feat_q.astype(jnp.float32)
    feat_kf = feat_k.astype(jnp.float32)
    value_f = value3.astype(jnp.float32)
    tail_mask = (docs == docs[-1]).astype(jnp.float32)
    head_mask = (docs == docs[0]).astype(jnp.float32)
    tail_state = jnp.einsum(
        "thf,thd->hfd",
        feat_k * tail_mask.astype(jnp.bfloat16)[:, None, None],
        value3,
        preferred_element_type=jnp.float32,
    )
    tail_norm = jnp.einsum("thf,t->hf", feat_kf, tail_mask, precision=HIGH)
    last_doc = doc_float[-1:]
    first_doc = doc_float[:1]
    head_feat = feat_qf * head_mask[:, None, None]
    state_shape = (H, F, DH)
    norm_shape = (H, F)
    forward_sums = prefix(pack_parts([last_doc, tail_state, tail_norm]), False, state_mover)
    pre_doc, state_in, norm_in = unpack_parts(forward_sums, [(1,), state_shape, norm_shape])
    pre_end = pre_doc[0]
    in_mask = (doc_float == pre_end).astype(jnp.float32)
    den = den_local + jnp.einsum("thf,hf->th", feat_qf, norm_in, precision=HIGH) * in_mask[:, None]
    scaled = grad3 / den[:, :, None]
    head_state = jnp.einsum("thf,thd->hfd", head_feat, scaled, precision=HIGH)
    in_mask, den, scaled, head_state = (in_mask, den, scaled, head_state)
    out = (
        num_local
        + jnp.einsum("thf,hfd->thd", feat_qf, state_in, precision=HIGH) * in_mask[:, None, None]
    ) / den[:, :, None]
    drift = -jnp.sum(grad3 * out, axis=2) / den
    head_norm = jnp.einsum("thf,th->hf", head_feat, drift, precision=HIGH)
    out, drift, head_norm = (out, drift, head_norm)
    backward_sums = prefix(pack_parts([first_doc, head_state, head_norm]), True, adjoint_mover)
    post_doc, adjoint, adjoint_norm = unpack_parts(backward_sums, [(1,), state_shape, norm_shape])
    suffix_doc = post_doc[0]
    scaled_b = scaled.astype(jnp.bfloat16)
    dscore = (
        jnp.einsum("thd,shd->hts", scaled_b, value3, preferred_element_type=jnp.float32)
        + drift.T[:, :, None]
    )
    dprobs = (dscore * mask[None]).astype(jnp.bfloat16)
    out_mask = (doc_float == suffix_doc).astype(jnp.float32)
    grad_fq = (
        jnp.einsum("hts,shf->thf", dprobs, feat_k, preferred_element_type=jnp.float32)
        + (
            jnp.einsum("hfd,thd->thf", state_in, scaled, precision=HIGH)
            + norm_in[None] * drift[:, :, None]
        )
        * in_mask[:, None, None]
    )
    grad_fk = (
        jnp.einsum("hts,thf->shf", dprobs, feat_q, preferred_element_type=jnp.float32)
        + (jnp.einsum("hfd,shd->shf", adjoint, value_f, precision=HIGH) + adjoint_norm[None])
        * out_mask[:, None, None]
    )
    value_grad = (
        jnp.einsum("hts,thd->shd", probs, scaled_b, preferred_element_type=jnp.float32)
        + jnp.einsum("shf,hfd->shd", feat_kf, adjoint, precision=HIGH) * out_mask[:, None, None]
    )
    grad_pq = (grad_fq * (1.0 + proj_q)).astype(jnp.bfloat16)
    grad_pk = (grad_fk * (1.0 + proj_k)).astype(jnp.bfloat16)
    query_grad = jnp.einsum("thf,df->thd", grad_pq, feat_weight, preferred_element_type=jnp.float32)
    key_grad = jnp.einsum("thf,df->thd", grad_pk, feat_weight, preferred_element_type=jnp.float32)
    weight_part = jnp.einsum(
        "thd,thf->df", query3, grad_pq, preferred_element_type=jnp.float32
    ) + jnp.einsum("thd,thf->df", key3, grad_pk, preferred_element_type=jnp.float32)
    weight_grad = lax.psum(weight_part, ("dp", "ctx"))
    scale = lax.rsqrt(jnp.mean(weight_grad * weight_grad) + EPSILON)
    new_weight = feat_weight.astype(jnp.float32) - RATE * weight_grad * scale
    shape_out = (1, tokens, H * DH)
    return (
        out.reshape(shape_out),
        query_grad.reshape(shape_out),
        key_grad.reshape(shape_out),
        value_grad.reshape(shape_out),
        new_weight,
    )


def solution(mesh):
    placed = (
        P("dp", "ctx", None),
        P("dp", "ctx", None),
        P("dp", "ctx", None),
        P("dp", "ctx"),
        P(),
        P("dp", "ctx", None),
    )
    return jax.shard_map(
        shards,
        mesh=mesh,
        in_specs=placed,
        out_specs=(
            P("dp", "ctx", None),
            P("dp", "ctx", None),
            P("dp", "ctx", None),
            P("dp", "ctx", None),
            P(),
        ),
        check_vma=False,
    )
```

profile of v0, /device:TPU:1, one launch (start us, length us, event | category | flops | bytes accessed | tf_op | source)
XLA Modules:
  0.0 1037.0 jit_solution(11877758748306444700)
XLA Ops:
  8.7 1.3 broadcast_compare_fusion
  14.5 10.6 %concatenate.51 = f32[330241]{0:T(1024)} concatenate(f32[1]{0:T(128)} %get-tuple-element.35, f32[327680]{0:T(1024)S(1)} %bitcast.136, f32[2560]{0:T(1024)S(1)} %convolution_reduce_fusion), dimensions={0} | concatenate | bytes 2641928 | tf_op jit(solution)/shard_map/concatenate | solution.py:27
  25.1 4.1 collective-permute-start
  29.2 27.9 %collective-permute-done = f32[330241]{0:T(1024)S(1)} collective-permute-done((f32[330241]{0:T(1024)}, f32[330241]{0:T(1024)S(1)}, u32[]{:S(2)}, u32[]{:S(2)}) %collective-permute-start) | collective-permute-done | bytes 1320996 | tf_op jit(solution)/shard_map/ppermute | solution.py:19
  58.2 4.1 collective-permute-start.1
  62.8 26.3 %collective-permute-done.1 = f32[330241]{0:T(1024)S(1)} collective-permute-done((f32[330241]{0:T(1024)S(1)}, f32[330241]{0:T(1024)S(1)}, u32[]{:S(2)}, u32[]{:S(2)}) %collective-permute-start.1) | collective-permute-done | bytes 1320996 | tf_op jit(solution)/shard_map/ppermute | solution.py:19
  93.3 6.8 collective-permute-start.2
  100.6 24.4 %collective-permute-done.2 = f32[330241]{0:T(1024)} collective-permute-done((f32[330241]{0:T(1024)S(1)}, f32[330241]{0:T(1024)}, u32[]{:S(2)}, u32[]{:S(2)}) %collective-permute-start.2) | collective-permute-done | bytes 1320996 | tf_op jit(solution)/shard_map/ppermute | solution.py:19
  127.5 2.1 fusion.27
  129.7 2.4 maximum_select_fusion.1
  132.1 9.4 collective-permute-start.3
  141.9 23.5 %collective-permute-done.3 = f32[330241]{0:T(1024)} collective-permute-done((f32[330241]{0:T(1024)S(1)}, f32[330241]{0:T(1024)}, u32[]{:S(2)}, u32[]{:S(2)}) %collective-permute-start.3) | collective-permute-done | bytes 1320996 | tf_op jit(solution)/shard_map/ppermute | solution.py:19
  167.9 2.1 fusion.26
  170.1 2.2 maximum_select_fusion.2
  172.3 5.6 collective-permute-start.4
  179.1 42.0 %collective-permute-done.4 = f32[330241]{0:T(1024)S(1)} collective-permute-done((f32[330241]{0:T(1024)}, f32[330241]{0:T(1024)S(1)}, u32[]{:S(2)}, u32[]{:S(2)}) %collective-permute-start.4) | collective-permute-done | bytes 1320996 | tf_op jit(solution)/shard_map/ppermute | solution.py:19
  222.9 2.1 fusion.25
  225.0 2.4 maximum_select_fusion.3
  227.4 25.8 %collective-permute-start.5 = (f32[330241]{0:T(1024)S(1)}, f32[330241]{0:T(1024)}, u32[]{:S(2)}, u32[]{:S(2)}) collective-permute-start(f32[330241]{0:T(1024)S(1)} %maximum_select_fusion.3), channel_id=1, source_target_pairs={{0,16},{1,17},{2,18},{3,19},{4,20},{5,21},{6,22},{7,23},{8,24},{9,... | collective-permute-start | bytes 3962900 | tf_op jit(solution)/shard_map/ppermute | solution.py:19
  253.7 33.4 %collective-permute-done.5 = f32[330241]{0:T(1024)} collective-permute-done((f32[330241]{0:T(1024)S(1)}, f32[330241]{0:T(1024)}, u32[]{:S(2)}, u32[]{:S(2)}) %collective-permute-start.5) | collective-permute-done | bytes 1320996 | tf_op jit(solution)/shard_map/ppermute | solution.py:19
  289.6 2.1 fusion.24
  291.7 2.2 maximum_select_fusion.4
  293.9 13.6 %collective-permute-start.6 = (f32[330241]{0:T(1024)}, f32[330241]{0:T(1024)S(1)}, u32[]{:S(2)}, u32[]{:S(2)}) collective-permute-start(f32[330241]{0:T(1024)} %maximum_select_fusion.4), channel_id=1, source_target_pairs={{0,32},{1,33},{2,34},{3,35},{4,36},{5,37},{6,38},{7,39},{8,40},{9,... | collective-permute-start | bytes 3962900 | tf_op jit(solution)/shard_map/ppermute | solution.py:19
  308.7 15.0 %collective-permute-done.6 = f32[330241]{0:T(1024)S(1)} collective-permute-done((f32[330241]{0:T(1024)}, f32[330241]{0:T(1024)S(1)}, u32[]{:S(2)}, u32[]{:S(2)}) %collective-permute-start.6) | collective-permute-done | bytes 1320996 | tf_op jit(solution)/shard_map/ppermute | solution.py:19
  325.5 2.1 fusion.23
  327.6 2.4 maximum_select_fusion.5
  330.0 33.4 %collective-permute-start.7 = (f32[330241]{0:T(1024)S(1)}, f32[330241]{0:T(1024)}, u32[]{:S(2)}, u32[]{:S(2)}) collective-permute-start(f32[330241]{0:T(1024)S(1)} %maximum_select_fusion.5), channel_id=1, source_target_pairs={{0,64},{1,65},{2,66},{3,67},{4,68},{5,69},{6,70},{7,71},{8,72},{9,... | collective-permute-start | bytes 3962900 | tf_op jit(solution)/shard_map/ppermute | solution.py:19
  363.4 2.0 copy.45
  365.4 2.2 copy.16
  367.7 2.5 fusion.30
  372.0 16.8 %collective-permute-done.7 = f32[330241]{0:T(1024)} collective-permute-done((f32[330241]{0:T(1024)S(1)}, f32[330241]{0:T(1024)}, u32[]{:S(2)}, u32[]{:S(2)}) %collective-permute-start.7) | collective-permute-done | bytes 1320996 | tf_op jit(solution)/shard_map/ppermute | solution.py:19
  391.4 2.1 fusion.22
  395.2 1.5 slice.320
  397.4 1.3 compare_convert_fusion.1
  398.7 3.4 fusion.12
  402.1 1.3 multiply_reduce_fusion
  403.5 3.4 fusion.36
  406.9 2.1 fusion.35
  409.1 13.9 %concatenate.59 = f32[330241]{0:T(1024)} concatenate(f32[1]{0:T(128)} %get-tuple-element.34, f32[327680]{0:T(1024)} %bitcast.149, f32[2560]{0:T(1024)S(1)} %reshape.197), dimensions={0} | concatenate | bytes 2641928 | tf_op jit(solution)/shard_map/concatenate | solution.py:27
  424.3 29.2 %collective-permute-done.8 = f32[330241]{0:T(1024)S(1)} collective-permute-done((f32[330241]{0:T(1024)}, f32[330241]{0:T(1024)S(1)}, u32[]{:S(2)}, u32[]{:S(2)}) %collective-permute-start.8) | collective-permute-done | bytes 1320996 | tf_op jit(solution)/shard_map/ppermute | solution.py:19
  456.4 27.6 %collective-permute-done.9 = f32[330241]{0:T(1024)S(1)} collective-permute-done((f32[330241]{0:T(1024)S(1)}, f32[330241]{0:T(1024)S(1)}, u32[]{:S(2)}, u32[]{:S(2)}) %collective-permute-start.9) | collective-permute-done | bytes 1320996 | tf_op jit(solution)/shard_map/ppermute | solution.py:19
  490.0 28.2 %collective-permute-done.10 = f32[330241]{0:T(1024)S(1)} collective-permute-done((f32[330241]{0:T(1024)S(1)}, f32[330241]{0:T(1024)S(1)}, u32[]{:S(2)}, u32[]{:S(2)}) %collective-permute-start.10) | collective-permute-done | bytes 1320996 | tf_op jit(solution)/shard_map/ppermute | solution.py:19
  522.0 1.5 collective-permute-start.11
  524.0 25.7 %collective-permute-done.11 = f32[330241]{0:T(1024)S(1)} collective-permute-done((f32[330241]{0:T(1024)S(1)}, f32[330241]{0:T(1024)S(1)}, u32[]{:S(2)}, u32[]{:S(2)}) %collective-permute-start.11) | collective-permute-done | bytes 1320996 | tf_op jit(solution)/shard_map/ppermute | solution.py:19
  555.1 56.0 %collective-permute-done.12 = f32[330241]{0:T(1024)S(1)} collective-permute-done((f32[330241]{0:T(1024)S(1)}, f32[330241]{0:T(1024)S(1)}, u32[]{:S(2)}, u32[]{:S(2)}) %collective-permute-start.12) | collective-permute-done | bytes 1320996 | tf_op jit(solution)/shard_map/ppermute | solution.py:19
  616.6 30.2 %collective-permute-done.13 = f32[330241]{0:T(1024)S(1)} collective-permute-done((f32[330241]{0:T(1024)S(1)}, f32[330241]{0:T(1024)S(1)}, u32[]{:S(2)}, u32[]{:S(2)}) %collective-permute-start.13) | collective-permute-done | bytes 1320996 | tf_op jit(solution)/shard_map/ppermute | solution.py:19
  651.9 4.2 fusion.7
  656.6 41.9 %collective-permute-done.14 = f32[330241]{0:T(1024)S(1)} collective-permute-done((f32[330241]{0:T(1024)S(1)}, f32[330241]{0:T(1024)S(1)}, u32[]{:S(2)}, u32[]{:S(2)}) %collective-permute-start.14) | collective-permute-done | bytes 1320996 | tf_op jit(solution)/shard_map/ppermute | solution.py:19
  702.3 1.6 collective-permute-start.15
  704.4 1.3 copy.28
  705.7 2.1 fusion.14
  707.8 1.3 fusion.63
  709.1 2.6 copy.29
  711.7 2.7 fusion.72
  714.4 1.5 fusion.56
  716.4 36.3 %collective-permute-done.15 = f32[330241]{0:T(1024)} collective-permute-done((f32[330241]{0:T(1024)S(1)}, f32[330241]{0:T(1024)}, u32[]{:S(2)}, u32[]{:S(2)}) %collective-permute-start.15) | collective-permute-done | bytes 1320996 | tf_op jit(solution)/shard_map/ppermute | solution.py:19
  755.2 2.1 fusion.15
  760.0 4.2 fusion.11
  764.3 1.4 fusion.13
  769.0 1.3 copy.31
  770.3 1.3 copy.30
  771.6 254.6 %all-reduce.2.cloned.1.call-done = f32[128,160]{0,1:T(8,128)} async-done(((f32[128,160]{0,1:T(8,128)}), f32[128,160]{0,1:T(8,128)}) %all-reduce.2.cloned.1.call-update) | async-done | bytes 81936 | tf_op jit(solution)/shard_map/psum | solution.py:161
  1026.2 1.5 multiply_reduce_fusion.1
  1028.4 1.5 multiply_subtract_fusion
  (159 shorter events, 59.3 us)
Async XLA Ops:
  7.2 5.4 copy-start.27
  7.2 5.5 copy-start.25
  7.2 1019.0 %all-reduce.2.cloned.1.call-start = ((), (), s32[]{:S(2)}) async-start(), calls=%async_computation | async-start | bytes 163840 | tf_op jit(solution)/shard_map/psum | solution.py:161
  12.5 0.9 copy-start.12
  12.7 1.2 copy-start.15
  13.4 1.1 copy-start.2
  14.5 42.7 %copy-start = (f32[330241]{0:T(1024)S(1)}, f32[330241]{0:T(1024)}, u32[]{:S(2)}) copy-start(f32[330241]{0:T(1024)} %constant.75.clone.1) | copy-start | bytes 3962896
  25.1 32.0 %collective-permute-start = (f32[330241]{0:T(1024)}, f32[330241]{0:T(1024)S(1)}, u32[]{:S(2)}, u32[]{:S(2)}) collective-permute-start(f32[330241]{0:T(1024)} %concatenate.51), channel_id=1, source_target_pairs={{0,1},{1,2},{2,3},{3,4},{4,5},{5,6},{6,7},{7,8},{8,9},{9,10},{10,1... | collective-permute-start | bytes 3962900 | tf_op jit(solution)/shard_map/ppermute | solution.py:19
  57.1 1.1 copy-start.7
  58.2 30.8 %collective-permute-start.1 = (f32[330241]{0:T(1024)S(1)}, f32[330241]{0:T(1024)S(1)}, u32[]{:S(2)}, u32[]{:S(2)}) collective-permute-start(f32[330241]{0:T(1024)S(1)} %broadcast_select_fusion.1), channel_id=1, source_target_pairs={{0,1},{1,2},{2,3},{3,4},{4,5},{5,6},{6,7},{7,8},{8,9},{9,10},{10,1... | collective-permute-start | bytes 3962900 | tf_op jit(solution)/shard_map/ppermute | solution.py:19
  90.9 1.3 copy-start.8
  93.3 34.2 %copy-start.1 = (f32[330241]{0:T(1024)}, f32[330241]{0:T(1024)S(1)}, u32[]{:S(2)}) copy-start(f32[330241]{0:T(1024)S(1)} %maximum_select_fusion) | copy-start | bytes 3962896
  93.3 31.7 %collective-permute-start.2 = (f32[330241]{0:T(1024)S(1)}, f32[330241]{0:T(1024)}, u32[]{:S(2)}, u32[]{:S(2)}) collective-permute-start(f32[330241]{0:T(1024)S(1)} %maximum_select_fusion), channel_id=1, source_target_pairs={{0,2},{1,3},{2,4},{3,5},{4,6},{5,7},{6,8},{7,9},{8,10},{9,11},{10,... | collective-permute-start | bytes 3962900 | tf_op jit(solution)/shard_map/ppermute | solution.py:19
  132.1 33.4 %collective-permute-start.3 = (f32[330241]{0:T(1024)S(1)}, f32[330241]{0:T(1024)}, u32[]{:S(2)}, u32[]{:S(2)}) collective-permute-start(f32[330241]{0:T(1024)S(1)} %maximum_select_fusion.1), channel_id=1, source_target_pairs={{0,4},{1,5},{2,6},{3,7},{4,8},{5,9},{6,10},{7,11},{8,12},{9,13},{1... | collective-permute-start | bytes 3962900 | tf_op jit(solution)/shard_map/ppermute | solution.py:19
  172.3 48.9 %collective-permute-start.4 = (f32[330241]{0:T(1024)}, f32[330241]{0:T(1024)S(1)}, u32[]{:S(2)}, u32[]{:S(2)}) collective-permute-start(f32[330241]{0:T(1024)} %maximum_select_fusion.2), channel_id=1, source_target_pairs={{0,8},{1,9},{2,10},{3,11},{4,12},{5,13},{6,14},{7,15},{8,16},{9,17... | collective-permute-start | bytes 3962900 | tf_op jit(solution)/shard_map/ppermute | solution.py:19
  227.4 59.7 %collective-permute-start.5 = (f32[330241]{0:T(1024)S(1)}, f32[330241]{0:T(1024)}, u32[]{:S(2)}, u32[]{:S(2)}) collective-permute-start(f32[330241]{0:T(1024)S(1)} %maximum_select_fusion.3), channel_id=1, source_target_pairs={{0,16},{1,17},{2,18},{3,19},{4,20},{5,21},{6,22},{7,23},{8,24},{9,... | collective-permute-start | bytes 3962900 | tf_op jit(solution)/shard_map/ppermute | solution.py:19
  293.9 29.8 %collective-permute-start.6 = (f32[330241]{0:T(1024)}, f32[330241]{0:T(1024)S(1)}, u32[]{:S(2)}, u32[]{:S(2)}) collective-permute-start(f32[330241]{0:T(1024)} %maximum_select_fusion.4), channel_id=1, source_target_pairs={{0,32},{1,33},{2,34},{3,35},{4,36},{5,37},{6,38},{7,39},{8,40},{9,... | collective-permute-start | bytes 3962900 | tf_op jit(solution)/shard_map/ppermute | solution.py:19
  330.0 58.8 %collective-permute-start.7 = (f32[330241]{0:T(1024)S(1)}, f32[330241]{0:T(1024)}, u32[]{:S(2)}, u32[]{:S(2)}) collective-permute-start(f32[330241]{0:T(1024)S(1)} %maximum_select_fusion.5), channel_id=1, source_target_pairs={{0,64},{1,65},{2,66},{3,67},{4,68},{5,69},{6,70},{7,71},{8,72},{9,... | collective-permute-start | bytes 3962900 | tf_op jit(solution)/shard_map/ppermute | solution.py:19
  367.7 3.8 copy-start.30
  370.2 18.7 %copy-start.4 = (bf16[128,16,160]{0,2,1:T(8,128)(2,1)}, bf16[128,16,160]{0,2,1:T(8,128)(2,1)S(1)}, u32[]{:S(2)}) copy-start(bf16[128,16,160]{0,2,1:T(8,128)(2,1)S(1)} %get-tuple-element.38) | copy-start | bytes 1966084
  395.2 1.6 copy-start.5
  398.7 3.4 copy-start.16
  398.7 3.4 copy-start.21
  398.7 3.4 copy-start.28
  402.1 249.8 %copy-start.32 = (f32[128,16]{0,1:T(8,128)}, f32[128,16]{0,1:T(8,128)S(1)}, u32[]{:S(2)}) copy-start(f32[128,16]{0,1:T(8,128)S(1)} %fusion.67) | copy-start | bytes 24580
  423.0 30.5 %collective-permute-start.8 = (f32[330241]{0:T(1024)}, f32[330241]{0:T(1024)S(1)}, u32[]{:S(2)}, u32[]{:S(2)}) collective-permute-start(f32[330241]{0:T(1024)} %concatenate.59), channel_id=1, source_target_pairs={{1,0},{2,1},{3,2},{4,3},{5,4},{6,5},{7,6},{8,7},{9,8},{10,9},{11,1... | collective-permute-start | bytes 3962900 | tf_op jit(solution)/shard_map/ppermute | solution.py:19
  453.5 1.1 copy-start.9
  454.6 29.4 %collective-permute-start.9 = (f32[330241]{0:T(1024)S(1)}, f32[330241]{0:T(1024)S(1)}, u32[]{:S(2)}, u32[]{:S(2)}) collective-permute-start(f32[330241]{0:T(1024)S(1)} %broadcast_select_fusion), channel_id=1, source_target_pairs={{1,0},{2,1},{3,2},{4,3},{5,4},{6,5},{7,6},{8,7},{9,8},{10,9},{11,1... | collective-permute-start | bytes 3962900 | tf_op jit(solution)/shard_map/ppermute | solution.py:19
  485.8 1.3 copy-start.10
  488.2 30.1 %collective-permute-start.10 = (f32[330241]{0:T(1024)S(1)}, f32[330241]{0:T(1024)S(1)}, u32[]{:S(2)}, u32[]{:S(2)}) collective-permute-start(f32[330241]{0:T(1024)S(1)} %maximum_select_fusion.7), channel_id=1, source_target_pairs={{2,0},{3,1},{4,2},{5,3},{6,4},{7,5},{8,6},{9,7},{10,8},{11,9},{12,... | collective-permute-start | bytes 3962900 | tf_op jit(solution)/shard_map/ppermute | solution.py:19
  522.0 27.7 %collective-permute-start.11 = (f32[330241]{0:T(1024)S(1)}, f32[330241]{0:T(1024)S(1)}, u32[]{:S(2)}, u32[]{:S(2)}) collective-permute-start(f32[330241]{0:T(1024)S(1)} %maximum_select_fusion.8), channel_id=1, source_target_pairs={{4,0},{5,1},{6,2},{7,3},{8,4},{9,5},{10,6},{11,7},{12,8},{13,9},{1... | collective-permute-start | bytes 3962900 | tf_op jit(solution)/shard_map/ppermute | solution.py:19
  553.3 57.8 %collective-permute-start.12 = (f32[330241]{0:T(1024)S(1)}, f32[330241]{0:T(1024)S(1)}, u32[]{:S(2)}, u32[]{:S(2)}) collective-permute-start(f32[330241]{0:T(1024)S(1)} %maximum_select_fusion.9), channel_id=1, source_target_pairs={{8,0},{9,1},{10,2},{11,3},{12,4},{13,5},{14,6},{15,7},{16,8},{17,9... | collective-permute-start | bytes 3962900 | tf_op jit(solution)/shard_map/ppermute | solution.py:19
  614.8 32.1 %collective-permute-start.13 = (f32[330241]{0:T(1024)S(1)}, f32[330241]{0:T(1024)S(1)}, u32[]{:S(2)}, u32[]{:S(2)}) collective-permute-start(f32[330241]{0:T(1024)S(1)} %maximum_select_fusion.10), channel_id=1, source_target_pairs={{16,0},{17,1},{18,2},{19,3},{20,4},{21,5},{22,6},{23,7},{24,8},{25... | collective-permute-start | bytes 3962900 | tf_op jit(solution)/shard_map/ppermute | solution.py:19
  650.5 48.0 %collective-permute-start.14 = (f32[330241]{0:T(1024)S(1)}, f32[330241]{0:T(1024)S(1)}, u32[]{:S(2)}, u32[]{:S(2)}) collective-permute-start(f32[330241]{0:T(1024)S(1)} %maximum_select_fusion.11), channel_id=1, source_target_pairs={{32,0},{33,1},{34,2},{35,3},{36,4},{37,5},{38,6},{39,7},{40,8},{41... | collective-permute-start | bytes 3962900 | tf_op jit(solution)/shard_map/ppermute | solution.py:19
  701.1 2.9 copy-start.17
  701.1 2.9 copy-start.22
  701.1 2.9 copy-start.31
  701.1 2.9 copy-start.33
  702.3 2.0 copy-start.24
  702.3 50.3 %collective-permute-start.15 = (f32[330241]{0:T(1024)S(1)}, f32[330241]{0:T(1024)}, u32[]{:S(2)}, u32[]{:S(2)}) collective-permute-start(f32[330241]{0:T(1024)S(1)} %maximum_select_fusion.12), channel_id=1, source_target_pairs={{64,0},{65,1},{66,2},{67,3},{68,4},{69,5},{70,6},{71,7},{72,8},{73... | collective-permute-start | bytes 3962900 | tf_op jit(solution)/shard_map/ppermute | solution.py:19
  704.3 3.4 copy-start.20
  705.7 2.1 copy-start.26
  709.1 2.6 copy-start.6
  711.7 2.7 copy-start.23
  711.7 2.7 copy-start.29
  711.7 2.7 copy-start.34
  760.0 4.2 copy-start.3
  760.0 4.2 copy-start.11
  760.0 4.2 copy-start.18
  764.3 1.4 copy-start.13
  765.7 1.0 copy-start.14
  767.7 1.2 copy-start.19
Sparse Core Ops, SparseCore 0:
  767.9 258.2 all-reduce.1
where the time goes:
time: 1050 us; the launch traced here: 1040 us
  waiting for transfers between devices  739 us (70%)
  starting transfers between devices  114 us (11%)
  local copies, waits for them, and re-layouts  66.3 us (6%)
  other arithmetic  49.1 us (5%)
  matrix products  35 us (3%)
  between operations  33.9 us (3%)
    ppermute x16, waiting for transfers between devices, passed_along(): return lax.ppermute(array, axis, pairs)  484 us
    psum x1, waiting for transfers between devices, shards(): weight_grad = lax.psum(weight_part, ('dp', 'ctx'))  255 us
    ppermute x16, starting transfers between devices, passed_along(): return lax.ppermute(array, axis, pairs)  114 us
    concatenate x2, local copies, waits for them, and re-layouts, pack_parts(): return jnp.concatenate([part.reshape(-1) for part in parts])  24.5 us
    select_n x14, other arithmetic, prefix(): total = jnp.where(valid(step), chain_combine(got, total), total)  21.1 us
  transfers between devices with their start and end apart: 17, of which 17 were waited for; matrix products, arithmetic and copies ran while one was open for 3% of the time, Pallas kernels for 0%

commit v1 on v0

--- a/solution.py
+++ b/solution.py
@@ -158,7 +158,7 @@
     weight_part = jnp.einsum(
         "thd,thf->df", query3, grad_pq, preferred_element_type=jnp.float32
     ) + jnp.einsum("thd,thf->df", key3, grad_pk, preferred_element_type=jnp.float32)
-    weight_grad = lax.psum(weight_part, ("dp", "ctx"))
+    weight_grad = jnp.sum(lax.all_gather(weight_part, ("dp", "ctx")), axis=0)
     scale = lax.rsqrt(jnp.mean(weight_grad * weight_grad) + EPSILON)
     new_weight = feat_weight.astype(jnp.float32) - RATE * weight_grad * scale
     shape_out = (1, tokens, H * DH)

time: 1050 us -> 958 us (0.912)
  waiting for transfers between devices: 739 us -> 632 us
  local copies, waits for them, and re-layouts: 66.3 us -> 79 us
  starting transfers between devices: 114 us -> 125 us
    psum x1 -> x0, waiting for transfers between devices: 255 us -> none  [shards(): weight_grad = lax.psum(weight_part, ('dp', 'ctx'))]
    all_gather x0 -> x1, waiting for transfers between devices: none -> 149 us  [shards(): weight_grad = jnp.sum(lax.all_gather(weight_part, ('dp', 'ctx')), axis=0)]
    unnamed x77 -> x62, local copies, waits for them, and re-layouts: 14.8 us -> 28.2 us
    ppermute x16, starting transfers between devices: 114 us -> 124 us  [passed_along(): return lax.ppermute(array, axis, pairs)]
  transfers between devices with their start and end apart: 17 -> 17, of which waited for: 17 -> 17; matrix products, arithmetic and copies ran while one was open for 3% -> 4% of each run, Pallas kernels for 0% -> 0%
where the time goes in v1:
time: 958 us; the launch traced here: 948 us
  waiting for transfers between devices  632 us (66%)
  starting transfers between devices  125 us (13%)
  local copies, waits for them, and re-layouts  79 us (8%)
  other arithmetic  48.2 us (5%)
  between operations  33.3 us (3%)
  matrix products  30.9 us (3%)
    ppermute x16, waiting for transfers between devices, passed_along(): return lax.ppermute(array, axis, pairs)  483 us
    all_gather x1, waiting for transfers between devices, shards(): weight_grad = jnp.sum(lax.all_gather(weight_part, ('dp', 'ctx')), axis=0)  149 us
    ppermute x16, starting transfers between devices, passed_along(): return lax.ppermute(array, axis, pairs)  124 us
    unnamed x62, local copies, waits for them, and re-layouts  28.2 us
    concatenate x2, local copies, waits for them, and re-layouts, pack_parts(): return jnp.concatenate([part.reshape(-1) for part in parts])  24.5 us
    select_n x14, other arithmetic, prefix(): total = jnp.where(valid(step), chain_combine(got, total), total)  20.9 us
  transfers between devices with their start and end apart: 17, of which 17 were waited for; matrix products, arithmetic and copies ran while one was open for 4% of the time, Pallas kernels for 0%

profile of v1, /device:TPU:1, one launch (start us, length us, event | category | flops | bytes accessed | tf_op | source)
XLA Modules:
  0.0 947.8 jit_solution(16744019342575722094)
XLA Ops:
  8.7 1.3 broadcast_compare_fusion
  14.4 10.6 %concatenate.51 = f32[330241]{0:T(1024)} concatenate(f32[1]{0:T(128)} %get-tuple-element.35, f32[327680]{0:T(1024)S(1)} %bitcast.142, f32[2560]{0:T(1024)S(1)} %convolution_reduce_fusion), dimensions={0} | concatenate | bytes 2641928 | tf_op jit(solution)/shard_map/concatenate | solution.py:27
  25.0 4.1 collective-permute-start
  29.1 27.9 %collective-permute-done = f32[330241]{0:T(1024)S(1)} collective-permute-done((f32[330241]{0:T(1024)}, f32[330241]{0:T(1024)S(1)}, u32[]{:S(2)}, u32[]{:S(2)}) %collective-permute-start) | collective-permute-done | bytes 1320996 | tf_op jit(solution)/shard_map/ppermute | solution.py:19
  58.1 4.1 collective-permute-start.1
  62.7 26.3 %collective-permute-done.1 = f32[330241]{0:T(1024)S(1)} collective-permute-done((f32[330241]{0:T(1024)S(1)}, f32[330241]{0:T(1024)S(1)}, u32[]{:S(2)}, u32[]{:S(2)}) %collective-permute-start.1) | collective-permute-done | bytes 1320996 | tf_op jit(solution)/shard_map/ppermute | solution.py:19
  93.2 6.8 collective-permute-start.2
  100.5 24.4 %collective-permute-done.2 = f32[330241]{0:T(1024)} collective-permute-done((f32[330241]{0:T(1024)S(1)}, f32[330241]{0:T(1024)}, u32[]{:S(2)}, u32[]{:S(2)}) %collective-permute-start.2) | collective-permute-done | bytes 1320996 | tf_op jit(solution)/shard_map/ppermute | solution.py:19
  127.4 2.1 fusion.27
  129.6 2.4 maximum_select_fusion.1
  132.0 9.3 collective-permute-start.3
  141.8 23.5 %collective-permute-done.3 = f32[330241]{0:T(1024)} collective-permute-done((f32[330241]{0:T(1024)S(1)}, f32[330241]{0:T(1024)}, u32[]{:S(2)}, u32[]{:S(2)}) %collective-permute-start.3) | collective-permute-done | bytes 1320996 | tf_op jit(solution)/shard_map/ppermute | solution.py:19
  167.8 2.1 fusion.26
  170.0 2.1 maximum_select_fusion.2
  172.1 5.6 collective-permute-start.4
  179.0 42.0 %collective-permute-done.4 = f32[330241]{0:T(1024)S(1)} collective-permute-done((f32[330241]{0:T(1024)}, f32[330241]{0:T(1024)S(1)}, u32[]{:S(2)}, u32[]{:S(2)}) %collective-permute-start.4) | collective-permute-done | bytes 1320996 | tf_op jit(solution)/shard_map/ppermute | solution.py:19
  222.8 2.1 fusion.25
  224.9 2.4 maximum_select_fusion.3
  227.3 25.8 %collective-permute-start.5 = (f32[330241]{0:T(1024)S(1)}, f32[330241]{0:T(1024)}, u32[]{:S(2)}, u32[]{:S(2)}) collective-permute-start(f32[330241]{0:T(1024)S(1)} %maximum_select_fusion.3), channel_id=1, source_target_pairs={{0,16},{1,17},{2,18},{3,19},{4,20},{5,21},{6,22},{7,23},{8,24},{9,... | collective-permute-start | bytes 3962900 | tf_op jit(solution)/shard_map/ppermute | solution.py:19
  253.6 33.4 %collective-permute-done.5 = f32[330241]{0:T(1024)} collective-permute-done((f32[330241]{0:T(1024)S(1)}, f32[330241]{0:T(1024)}, u32[]{:S(2)}, u32[]{:S(2)}) %collective-permute-start.5) | collective-permute-done | bytes 1320996 | tf_op jit(solution)/shard_map/ppermute | solution.py:19
  289.4 2.1 fusion.24
  291.6 2.1 maximum_select_fusion.4
  293.7 13.6 %collective-permute-start.6 = (f32[330241]{0:T(1024)}, f32[330241]{0:T(1024)S(1)}, u32[]{:S(2)}, u32[]{:S(2)}) collective-permute-start(f32[330241]{0:T(1024)} %maximum_select_fusion.4), channel_id=1, source_target_pairs={{0,32},{1,33},{2,34},{3,35},{4,36},{5,37},{6,38},{7,39},{8,40},{9,... | collective-permute-start | bytes 3962900 | tf_op jit(solution)/shard_map/ppermute | solution.py:19
  308.6 15.0 %collective-permute-done.6 = f32[330241]{0:T(1024)S(1)} collective-permute-done((f32[330241]{0:T(1024)}, f32[330241]{0:T(1024)S(1)}, u32[]{:S(2)}, u32[]{:S(2)}) %collective-permute-start.6) | collective-permute-done | bytes 1320996 | tf_op jit(solution)/shard_map/ppermute | solution.py:19
  325.4 2.1 fusion.23
  327.4 2.4 maximum_select_fusion.5
  329.8 44.6 %collective-permute-start.7 = (f32[330241]{0:T(1024)S(1)}, f32[330241]{0:T(1024)}, u32[]{:S(2)}, u32[]{:S(2)}) collective-permute-start(f32[330241]{0:T(1024)S(1)} %maximum_select_fusion.5), channel_id=1, source_target_pairs={{0,64},{1,65},{2,66},{3,67},{4,68},{5,69},{6,70},{7,71},{8,72},{9,... | collective-permute-start | bytes 3962900 | tf_op jit(solution)/shard_map/ppermute | solution.py:19
  374.4 2.0 copy.45
  376.4 2.2 copy.16
  378.7 2.5 fusion.30
  381.2 1.3 convert_reduce_fusion
  383.0 5.6 collective-permute-done.7
  391.1 2.1 fusion.22
  394.8 1.5 slice.320
  398.2 3.4 fusion.12
  401.6 1.3 multiply_reduce_fusion
  403.0 3.4 fusion.36
  406.4 2.1 fusion.35
  408.6 13.9 %concatenate.59 = f32[330241]{0:T(1024)} concatenate(f32[1]{0:T(128)} %get-tuple-element.34, f32[327680]{0:T(1024)} %bitcast.155, f32[2560]{0:T(1024)S(1)} %reshape.197), dimensions={0} | concatenate | bytes 2641928 | tf_op jit(solution)/shard_map/concatenate | solution.py:27
  423.8 29.2 %collective-permute-done.8 = f32[330241]{0:T(1024)S(1)} collective-permute-done((f32[330241]{0:T(1024)}, f32[330241]{0:T(1024)S(1)}, u32[]{:S(2)}, u32[]{:S(2)}) %collective-permute-start.8) | collective-permute-done | bytes 1320996 | tf_op jit(solution)/shard_map/ppermute | solution.py:19
  455.9 27.6 %collective-permute-done.9 = f32[330241]{0:T(1024)S(1)} collective-permute-done((f32[330241]{0:T(1024)S(1)}, f32[330241]{0:T(1024)S(1)}, u32[]{:S(2)}, u32[]{:S(2)}) %collective-permute-start.9) | collective-permute-done | bytes 1320996 | tf_op jit(solution)/shard_map/ppermute | solution.py:19
  487.6 1.3 collective-permute-start.10
  489.4 28.3 %collective-permute-done.10 = f32[330241]{0:T(1024)S(1)} collective-permute-done((f32[330241]{0:T(1024)S(1)}, f32[330241]{0:T(1024)S(1)}, u32[]{:S(2)}, u32[]{:S(2)}) %collective-permute-start.10) | collective-permute-done | bytes 1320996 | tf_op jit(solution)/shard_map/ppermute | solution.py:19
  523.1 25.9 %collective-permute-done.11 = f32[330241]{0:T(1024)S(1)} collective-permute-done((f32[330241]{0:T(1024)S(1)}, f32[330241]{0:T(1024)S(1)}, u32[]{:S(2)}, u32[]{:S(2)}) %collective-permute-start.11) | collective-permute-done | bytes 1320996 | tf_op jit(solution)/shard_map/ppermute | solution.py:19
  554.3 55.9 %collective-permute-done.12 = f32[330241]{0:T(1024)S(1)} collective-permute-done((f32[330241]{0:T(1024)S(1)}, f32[330241]{0:T(1024)S(1)}, u32[]{:S(2)}, u32[]{:S(2)}) %collective-permute-start.12) | collective-permute-done | bytes 1320996 | tf_op jit(solution)/shard_map/ppermute | solution.py:19
  613.9 1.3 collective-permute-start.13
  615.7 30.3 %collective-permute-done.13 = f32[330241]{0:T(1024)S(1)} collective-permute-done((f32[330241]{0:T(1024)S(1)}, f32[330241]{0:T(1024)S(1)}, u32[]{:S(2)}, u32[]{:S(2)}) %collective-permute-start.13) | collective-permute-done | bytes 1320996 | tf_op jit(solution)/shard_map/ppermute | solution.py:19
  651.4 46.1 %collective-permute-done.14 = f32[330241]{0:T(1024)S(1)} collective-permute-done((f32[330241]{0:T(1024)S(1)}, f32[330241]{0:T(1024)S(1)}, u32[]{:S(2)}, u32[]{:S(2)}) %collective-permute-start.14) | collective-permute-done | bytes 1320996 | tf_op jit(solution)/shard_map/ppermute | solution.py:19
  701.0 1.5 collective-permute-start.15
  702.6 1.8 fusion.37
  704.4 1.6 fusion.72
  706.4 1.6 fusion.7
  709.7 41.4 %collective-permute-done.15 = f32[330241]{0:T(1024)S(1)} collective-permute-done((f32[330241]{0:T(1024)S(1)}, f32[330241]{0:T(1024)S(1)}, u32[]{:S(2)}, u32[]{:S(2)}) %collective-permute-start.15) | collective-permute-done | bytes 1320996 | tf_op jit(solution)/shard_map/ppermute | solution.py:19
  756.8 2.9 fusion.13
  762.7 2.5 copy.28
  765.2 1.3 fusion.63
  766.6 2.6 copy.29
  769.2 1.5 fusion.56
  770.7 1.9 fusion.11
  772.6 1.3 copy.31
  774.3 1.3 copy.30
  775.6 149.1 %all-gather.3.cloned.1.call-done = f32[32768,160]{0,1:T(8,128)} async-done(((f32[128,160]{0,1:T(8,128)}), f32[32768,160]{0,1:T(8,128)}) %all-gather.3.cloned.1.call-update) | async-done | bytes 20971536 | tf_op jit(solution)/shard_map/all_gather | solution.py:161
  924.6 11.5 %copy.47 = f32[20,8,256,128]{3,2,1,0:T(8,128)S(1)} copy(f32[20,8,256,128]{3,1,2,0:T(8,128)} %bitcast.137) | data formatting | bytes 41943040
  936.1 2.5 bitcast_reduce_fusion
  (145 shorter events, 60.7 us)
Async XLA Ops:
  7.2 5.4 copy-start.25
  7.2 5.5 copy-start.24
  7.2 917.5 %all-gather.3.cloned.1.call-start = ((), (), s32[]{:S(2)}) async-start(), calls=%async_computation | async-start | bytes 21053440 | tf_op jit(solution)/shard_map/all_gather | solution.py:161
  12.5 0.8 copy-start.16
  12.7 1.2 copy-start.19
  13.3 1.1 copy-start.2
  14.4 42.7 %copy-start = (f32[330241]{0:T(1024)S(1)}, f32[330241]{0:T(1024)}, u32[]{:S(2)}) copy-start(f32[330241]{0:T(1024)} %constant.75.clone.1) | copy-start | bytes 3962896
  25.0 32.0 %collective-permute-start = (f32[330241]{0:T(1024)}, f32[330241]{0:T(1024)S(1)}, u32[]{:S(2)}, u32[]{:S(2)}) collective-permute-start(f32[330241]{0:T(1024)} %concatenate.51), channel_id=1, source_target_pairs={{0,1},{1,2},{2,3},{3,4},{4,5},{5,6},{6,7},{7,8},{8,9},{9,10},{10,1... | collective-permute-start | bytes 3962900 | tf_op jit(solution)/shard_map/ppermute | solution.py:19
  57.1 1.1 copy-start.10
  58.1 30.8 %collective-permute-start.1 = (f32[330241]{0:T(1024)S(1)}, f32[330241]{0:T(1024)S(1)}, u32[]{:S(2)}, u32[]{:S(2)}) collective-permute-start(f32[330241]{0:T(1024)S(1)} %broadcast_select_fusion.1), channel_id=1, source_target_pairs={{0,1},{1,2},{2,3},{3,4},{4,5},{5,6},{6,7},{7,8},{8,9},{9,10},{10,1... | collective-permute-start | bytes 3962900 | tf_op jit(solution)/shard_map/ppermute | solution.py:19
  90.8 1.3 copy-start.11
  93.2 34.2 %copy-start.1 = (f32[330241]{0:T(1024)}, f32[330241]{0:T(1024)S(1)}, u32[]{:S(2)}) copy-start(f32[330241]{0:T(1024)S(1)} %maximum_select_fusion) | copy-start | bytes 3962896
  93.2 31.7 %collective-permute-start.2 = (f32[330241]{0:T(1024)S(1)}, f32[330241]{0:T(1024)}, u32[]{:S(2)}, u32[]{:S(2)}) collective-permute-start(f32[330241]{0:T(1024)S(1)} %maximum_select_fusion), channel_id=1, source_target_pairs={{0,2},{1,3},{2,4},{3,5},{4,6},{5,7},{6,8},{7,9},{8,10},{9,11},{10,... | collective-permute-start | bytes 3962900 | tf_op jit(solution)/shard_map/ppermute | solution.py:19
  132.0 33.4 %collective-permute-start.3 = (f32[330241]{0:T(1024)S(1)}, f32[330241]{0:T(1024)}, u32[]{:S(2)}, u32[]{:S(2)}) collective-permute-start(f32[330241]{0:T(1024)S(1)} %maximum_select_fusion.1), channel_id=1, source_target_pairs={{0,4},{1,5},{2,6},{3,7},{4,8},{5,9},{6,10},{7,11},{8,12},{9,13},{1... | collective-permute-start | bytes 3962900 | tf_op jit(solution)/shard_map/ppermute | solution.py:19
  172.1 48.9 %collective-permute-start.4 = (f32[330241]{0:T(1024)}, f32[330241]{0:T(1024)S(1)}, u32[]{:S(2)}, u32[]{:S(2)}) collective-permute-start(f32[330241]{0:T(1024)} %maximum_select_fusion.2), channel_id=1, source_target_pairs={{0,8},{1,9},{2,10},{3,11},{4,12},{5,13},{6,14},{7,15},{8,16},{9,17... | collective-permute-start | bytes 3962900 | tf_op jit(solution)/shard_map/ppermute | solution.py:19
  227.3 59.7 %collective-permute-start.5 = (f32[330241]{0:T(1024)S(1)}, f32[330241]{0:T(1024)}, u32[]{:S(2)}, u32[]{:S(2)}) collective-permute-start(f32[330241]{0:T(1024)S(1)} %maximum_select_fusion.3), channel_id=1, source_target_pairs={{0,16},{1,17},{2,18},{3,19},{4,20},{5,21},{6,22},{7,23},{8,24},{9,... | collective-permute-start | bytes 3962900 | tf_op jit(solution)/shard_map/ppermute | solution.py:19
  293.7 29.8 %collective-permute-start.6 = (f32[330241]{0:T(1024)}, f32[330241]{0:T(1024)S(1)}, u32[]{:S(2)}, u32[]{:S(2)}) collective-permute-start(f32[330241]{0:T(1024)} %maximum_select_fusion.4), channel_id=1, source_target_pairs={{0,32},{1,33},{2,34},{3,35},{4,36},{5,37},{6,38},{7,39},{8,40},{9,... | collective-permute-start | bytes 3962900 | tf_op jit(solution)/shard_map/ppermute | solution.py:19
  329.8 58.8 %collective-permute-start.7 = (f32[330241]{0:T(1024)S(1)}, f32[330241]{0:T(1024)}, u32[]{:S(2)}, u32[]{:S(2)}) collective-permute-start(f32[330241]{0:T(1024)S(1)} %maximum_select_fusion.5), channel_id=1, source_target_pairs={{0,64},{1,65},{2,66},{3,67},{4,68},{5,69},{6,70},{7,71},{8,72},{9,... | collective-permute-start | bytes 3962900 | tf_op jit(solution)/shard_map/ppermute | solution.py:19
  381.2 7.5 copy-start.4
  394.8 1.6 copy-start.5
  398.2 3.4 copy-start.20
  398.2 3.4 copy-start.21
  398.2 3.4 copy-start.26
  422.5 30.5 %collective-permute-start.8 = (f32[330241]{0:T(1024)}, f32[330241]{0:T(1024)S(1)}, u32[]{:S(2)}, u32[]{:S(2)}) collective-permute-start(f32[330241]{0:T(1024)} %concatenate.59), channel_id=1, source_target_pairs={{1,0},{2,1},{3,2},{4,3},{5,4},{6,5},{7,6},{8,7},{9,8},{10,9},{11,1... | collective-permute-start | bytes 3962900 | tf_op jit(solution)/shard_map/ppermute | solution.py:19
  453.0 1.1 copy-start.12
  454.1 29.4 %collective-permute-start.9 = (f32[330241]{0:T(1024)S(1)}, f32[330241]{0:T(1024)S(1)}, u32[]{:S(2)}, u32[]{:S(2)}) collective-permute-start(f32[330241]{0:T(1024)S(1)} %broadcast_select_fusion), channel_id=1, source_target_pairs={{1,0},{2,1},{3,2},{4,3},{5,4},{6,5},{7,6},{8,7},{9,8},{10,9},{11,1... | collective-permute-start | bytes 3962900 | tf_op jit(solution)/shard_map/ppermute | solution.py:19
  485.2 1.3 copy-start.13
  487.6 30.1 %collective-permute-start.10 = (f32[330241]{0:T(1024)S(1)}, f32[330241]{0:T(1024)S(1)}, u32[]{:S(2)}, u32[]{:S(2)}) collective-permute-start(f32[330241]{0:T(1024)S(1)} %maximum_select_fusion.7), channel_id=1, source_target_pairs={{2,0},{3,1},{4,2},{5,3},{6,4},{7,5},{8,6},{9,7},{10,8},{11,9},{12,... | collective-permute-start | bytes 3962900 | tf_op jit(solution)/shard_map/ppermute | solution.py:19
  521.3 27.7 %collective-permute-start.11 = (f32[330241]{0:T(1024)S(1)}, f32[330241]{0:T(1024)S(1)}, u32[]{:S(2)}, u32[]{:S(2)}) collective-permute-start(f32[330241]{0:T(1024)S(1)} %maximum_select_fusion.8), channel_id=1, source_target_pairs={{4,0},{5,1},{6,2},{7,3},{8,4},{9,5},{10,6},{11,7},{12,8},{13,9},{1... | collective-permute-start | bytes 3962900 | tf_op jit(solution)/shard_map/ppermute | solution.py:19
  552.5 57.7 %collective-permute-start.12 = (f32[330241]{0:T(1024)S(1)}, f32[330241]{0:T(1024)S(1)}, u32[]{:S(2)}, u32[]{:S(2)}) collective-permute-start(f32[330241]{0:T(1024)S(1)} %maximum_select_fusion.9), channel_id=1, source_target_pairs={{8,0},{9,1},{10,2},{11,3},{12,4},{13,5},{14,6},{15,7},{16,8},{17,9... | collective-permute-start | bytes 3962900 | tf_op jit(solution)/shard_map/ppermute | solution.py:19
  613.9 32.1 %collective-permute-start.13 = (f32[330241]{0:T(1024)S(1)}, f32[330241]{0:T(1024)S(1)}, u32[]{:S(2)}, u32[]{:S(2)}) collective-permute-start(f32[330241]{0:T(1024)S(1)} %maximum_select_fusion.10), channel_id=1, source_target_pairs={{16,0},{17,1},{18,2},{19,3},{20,4},{21,5},{22,6},{23,7},{24,8},{25... | collective-permute-start | bytes 3962900 | tf_op jit(solution)/shard_map/ppermute | solution.py:19
  649.5 47.9 %collective-permute-start.14 = (f32[330241]{0:T(1024)S(1)}, f32[330241]{0:T(1024)S(1)}, u32[]{:S(2)}, u32[]{:S(2)}) collective-permute-start(f32[330241]{0:T(1024)S(1)} %maximum_select_fusion.11), channel_id=1, source_target_pairs={{32,0},{33,1},{34,2},{35,3},{36,4},{37,5},{38,6},{39,7},{40,8},{41... | collective-permute-start | bytes 3962900 | tf_op jit(solution)/shard_map/ppermute | solution.py:19
  701.0 50.1 %collective-permute-start.15 = (f32[330241]{0:T(1024)S(1)}, f32[330241]{0:T(1024)S(1)}, u32[]{:S(2)}, u32[]{:S(2)}) collective-permute-start(f32[330241]{0:T(1024)S(1)} %maximum_select_fusion.12), channel_id=1, source_target_pairs={{64,0},{65,1},{66,2},{67,3},{68,4},{69,5},{70,6},{71,7},{72,8},{73... | collective-permute-start | bytes 3962900 | tf_op jit(solution)/shard_map/ppermute | solution.py:19
  702.6 1.8 copy-start.6
  704.4 1.6 copy-start.14
  704.4 2.0 copy-start.22
  706.4 1.6 copy-start.15
  755.4 1.3 copy-start.3
  756.7 3.7 copy-start.17
  759.6 0.9 copy-start.8
  760.5 1.1 copy-start.7
  760.5 1.2 copy-start.18
  766.6 2.6 copy-start.23
  772.6 1.3 copy-start.9
Sparse Core Ops, SparseCore 0:
  762.8 161.7 all-gather.2
